TPU v7x, 32 devices: a whole 2x2x4 slice. The times are simulated.
32 devices in a mesh: slab: 8 (over z, y), mode: 4 (over x, core).
Axes of the slice: x: 2, y: 2, z: 4, core: 2. Of those that a mesh axis runs over, the one named last changes fastest.
Arguments:
- eigvec: bfloat16 [10240, 3, 1024], P('slab', None, 'mode'), may hold values from -6 to 6
- species: int32 [10240], P('slab'), may hold values from 0 to 3
- mode_cot: float32 [1024], P('mode'), may hold values from -4 to 4
- neighbours: int32 [10240, 16], P('slab'), may hold values from 0 to 2560, as said below
- pair_features: bfloat16 [163840, 128], P(('slab', 'mode')), may hold values from -130 to 130
- w_in: bfloat16 [128, 256], replicated, may hold values from -0.5 to 0.5
- b_in: float32 [256], replicated, may hold values from -3 to 3
- w_out: bfloat16 [9, 256], replicated, may hold values from -0.375 to 0.375
Outputs:
- features_grad: bfloat16 [163840, 128], P(('slab', 'mode'))
- grad_w_in: float32 [128, 256], replicated
- grad_b_in: float32 [256], replicated
- grad_w_out: float32 [9, 256], replicated
Inputs may be any that keep to these rules, and one draw needn't show every extreme that they name: `neighbours`: atom r of a slab (0 to 1279) lists extended indices from r to r + 1280; extended index x stands for atom (slab * 1280 + x - 640) mod 10240; the value 1280 + 2 * 640 marks an empty slot.
All inputs are finite; a program needn't handle non-finite values.
Results may differ from a plain program's by a relative error of at most 0.019.
Values may be sent and summed in bfloat16 or wider, within the bound.
A program may use at most 64 MiB of HBM per device.

v0:
```python
import functools
import math

import jax
import jax.numpy as jnp
from jax import lax
from jax.experimental import pallas as pl
from jax.experimental.pallas import tpu as pltpu
from jax.sharding import PartitionSpec as P

MASS_TABLE = (1.35, 2.94, 2.79, 2.95)
CLIP_NORM = 100.0
TILE = 128
VMEM_LIMIT = 62 * 1024 * 1024
MESH = pl.DeviceIdType.MESH
VMEM = pl.BlockSpec(memory_space=pltpu.VMEM)
ANY = pl.BlockSpec(memory_space=pl.ANY)


def rows_of(block):
    return pl.ds(pl.multiple_of(block * TILE, TILE), TILE)


def kernel(slabs, groups, eig_ref, species_ref, cot_ref, nbr_ref, x_hbm, w_in_ref, b_in_ref, w_out_ref,
           grad_ref, everyone,
           eig, x_ref, species_row, w_rep_ref, panel, weighted, nbr_in, low_ref, high_ref, even, odd, firsts, lasts, outgoing,
           own_in, far_in, forward, returned, total_first, total_last, hidden_ref, slope_ref, pre_ref,
           w_out_sum, sums, sums_out, near_in, mine, rounds, summed,
           eig_sem, x_sem, rim_send, rim_recv, nbr_send, nbr_recv, pair_send, own_recv, far_recv,
           forward_send, returned_recv, near_send, near_recv, slab_send, slab_recv, back_send, back_recv):
    slab, mode = lax.axis_index("slab"), lax.axis_index("mode")
    atoms = eig.shape[1]
    slot_count = nbr_ref.shape[0]
    blocks = atoms // TILE
    rim = blocks // 2
    eights = TILE // 8
    sentinel = 2 * atoms
    share = atoms // groups
    fold = 8 * TILE // slot_count
    features = x_ref.shape[1]
    quarter = mine.shape[0]

    def blocks_of(owner):
        return list(range(owner * share // TILE, -(-(owner + 1) * share // TILE)))

    width = max(len(blocks_of(owner)) for owner in range(groups))
    owned = {block: [(owner, blocks_of(owner).index(block)) for owner in range(groups) if block in blocks_of(owner)]
             for block in range(blocks)}

    def peer_mode(hop):
        return lax.rem(mode + hop, groups)

    def peer_slab(hop):
        return lax.rem(slab + hop, slabs)

    previous, following = peer_slab(slabs - 1), peer_slab(1)

    eig_copies = [pltpu.make_async_copy(
        eig_ref.at[:, block * TILE : (block + 1) * TILE, :], eig.at[:, block * TILE : (block + 1) * TILE, :],
        eig_sem.at[block]) for block in range(rim)]
    eig_copies.append(pltpu.make_async_copy(
        eig_ref.at[:, rim * TILE :, :], eig.at[:, rim * TILE :, :], eig_sem.at[rim]))
    for copy in eig_copies:
        copy.start()
    x_copy = pltpu.make_async_copy(x_hbm, x_ref, x_sem.at[0])
    x_copy.start()

    barrier = pltpu.get_barrier_semaphore()
    for hop in range(1, groups):
        pl.semaphore_signal(barrier, inc=1, device_id=(slab, peer_mode(hop)), device_id_type=MESH)

    def greet(hop, _):
        pl.semaphore_signal(barrier, inc=1, device_id=(peer_slab(hop), mode), device_id_type=MESH)
        return 0

    lax.fori_loop(1, slabs, greet, 0)
    species_row[...] = species_ref[...].reshape(species_row.shape)
    roots = [1.0 / math.sqrt(mass) for mass in MASS_TABLE]

    def scale(block):
        kinds = jnp.transpose(jnp.broadcast_to(
            species_row[:, rows_of(block)], (TILE, TILE)))
        root = jnp.full((TILE, TILE), roots[0], jnp.float32)
        for kind in range(1, len(roots)):
            root = jnp.where(kinds == kind, roots[kind], root)
        root = jnp.concatenate([root] * (eig.shape[2] // TILE), axis=1)
        for a in range(3):
            panel[a, rows_of(block), :] = (eig[a, rows_of(block), :].astype(jnp.float32) * root).astype(jnp.bfloat16)

    def weigh(block):
        for a in range(3):
            weighted[a, rows_of(block), :] = (
                panel[a, rows_of(block), :].astype(jnp.float32) * cot_ref[...]).astype(jnp.bfloat16)

    def tables(slots, base, block):
        spread = jnp.transpose(jnp.concatenate([slots] * (TILE // slot_count), axis=0))
        offset = spread - base * TILE
        low_ref[rows_of(block), :] = offset & (TILE - 1)
        high_ref[rows_of(block), :] = lax.shift_right_arithmetic(offset, 7)

    rim_copies = [pltpu.make_async_remote_copy(
        src_ref=panel.at[:, q * TILE : (q + 1) * TILE, :],
        dst_ref=panel.at[:, (blocks + q) * TILE : (blocks + q + 1) * TILE, :],
        send_sem=rim_send.at[q], recv_sem=rim_recv.at[q],
        device_id=(previous, mode), device_id_type=MESH) for q in range(rim)]
    nbr_copy = pltpu.make_async_remote_copy(
        src_ref=nbr_ref.at[:, 0 : rim * TILE], dst_ref=nbr_in, send_sem=nbr_send.at[0], recv_sem=nbr_recv.at[0],
        device_id=(previous, mode), device_id_type=MESH)

    eig_copies[0].wait()
    scale(0)
    pl.semaphore_wait(barrier, groups - 1 + slabs - 1)
    rim_copies[0].start()
    nbr_copy.start()
    for q in range(1, rim):
        eig_copies[q].wait()
        scale(q)
        rim_copies[q].start()
    eig_copies[rim].wait()

    def begin(block, _):
        scale(block)
        return 0

    lax.fori_loop(rim, blocks, begin, 0)

    def ready(block, _):
        weigh(block)
        tables(nbr_ref[:, rows_of(block)], block, block)
        return 0

    lax.fori_loop(0, blocks, ready, 0)

    prods = (even, odd)

    def product(buffer, tile, left_block, right_block):
        left = jnp.concatenate([weighted[a, rows_of(left_block), :] for a in range(3)], axis=0)
        right = jnp.concatenate([panel[b, rows_of(right_block), :] for b in range(3)], axis=0)
        prods[buffer][tile] = lax.dot_general(
            left, right, (((1,), (1,)), ((), ())), preferred_element_type=jnp.float32)

    position = lax.broadcasted_iota(jnp.int32, (8, TILE), 1) // slot_count

    def pick(buffer, eight, block, entries, diagonal):
        rows = pl.ds(pl.multiple_of(block * TILE + 8 * eight, 8), 8)
        lane, high = low_ref[rows, :], high_ref[rows, :]
        hits = [high == distance for _, distance in entries]
        first = jnp.zeros((8, TILE), jnp.float32)
        if diagonal is not None:
            live = (high * TILE + lane + block * TILE) < sentinel
            same = lax.broadcasted_iota(jnp.int32, (8, TILE), 0) + 8 * eight
        for part in range(9):
            a, b = part // 3, part % 3
            piece = pl.ds(pl.multiple_of(a * TILE + 8 * eight, 8), 8)
            picked = jnp.zeros((8, TILE), jnp.float32)
            for (tile, _), hit in zip(entries, hits):
                values = prods[buffer][tile, piece, b * TILE : (b + 1) * TILE]
                picked = jnp.where(
                    hit, jnp.take_along_axis(values, lane, axis=1, mode="promise_in_bounds"), picked)
            if diagonal is not None:
                values = prods[buffer][diagonal, piece, b * TILE : (b + 1) * TILE]
                own = jnp.take_along_axis(values, same, axis=1, mode="promise_in_bounds")
                picked = jnp.where(live, picked - own, 0.0)
            if part < 8:
                first = jnp.where(position == part, picked, first)
        return rows, first, picked

    tiles = 3 * rim + 1
    assert tiles == eights

    def own_product(pair, tile):
        second = (tile + 2 * rim - pair) // tiles
        product(pair % 2, tile, pair + rim * second, tile - (rim + 1) * second)

    def own_pick(pair, eight):
        for block, entries, diagonal in (
            (pair, [(t, t - pair + rim) for t in range(rim + 1 + pair)], pair),
            (pair + rim, [(rim + 1 + pair + t, t) for t in range(2 * rim - pair)], 2 * rim + 1 + pair),
        ):
            rows, first, last = pick(pair % 2, eight, block, entries, diagonal)
            firsts[rows, :] = first
            lasts[rows, :] = last

    def lead(tile, _):
        own_product(0, tile)
        return 0

    lax.fori_loop(0, tiles, lead, 0)
    for pair in range(rim):
        def own_step(step, _):
            for half in range(2):
                own_pick(pair, 2 * step + half)
                if pair + 1 < rim:
                    own_product(pair + 1, 2 * step + half)
            return 0

        lax.fori_loop(0, tiles // 2, own_step, 0)

    def pack(block):
        outgoing[block, 0:TILE, :] = firsts[rows_of(block), :].astype(jnp.bfloat16)
        folds = []
        for unit in range(TILE // fold):
            folded = jnp.zeros((8, TILE), jnp.float32)
            for p in range(fold // 8):
                folded = jnp.where(
                    position == p, lasts[pl.ds(block * TILE + unit * fold + 8 * p, 8), :], folded)
            folds.append(folded)
        outgoing[block, TILE:, :] = jnp.concatenate(folds, axis=0).astype(jnp.bfloat16)

    def pair_copy(block, index, owner, place, hop):
        target, sems = (own_in, own_recv) if block < blocks else (far_in, far_recv)
        return pltpu.make_async_remote_copy(
            src_ref=outgoing.at[block], dst_ref=target.at[hop, place], send_sem=pair_send.at[block, index],
            recv_sem=sems.at[hop, place], device_id=(slab, owner), device_id_type=MESH)

    def deliver(block, action):
        for index, (owner, place) in enumerate(owned[block % blocks]):
            @pl.when(mode != owner)
            def _():
                copy = pair_copy(block, index, owner, place, lax.rem(mode - owner + groups, groups) - 1)
                if action == "start":
                    copy.start()
                else:
                    copy.wait_send()

    for block in range(rim):
        pack(block)
        deliver(block, "start")

    for part in range(8):
        w_rep_ref[part * slot_count : (part + 1) * slot_count, :] = jnp.broadcast_to(
            w_out_ref[part : part + 1, :].astype(jnp.float32), (slot_count, w_rep_ref.shape[1])).astype(jnp.bfloat16)
    w_rep_ref[TILE:, :] = jnp.broadcast_to(
        w_out_ref[8:9, :].astype(jnp.float32), (TILE, w_rep_ref.shape[1])).astype(jnp.bfloat16)
    x_copy.wait()
    unit_rows = fold * slot_count
    units = share // fold

    def before(unit, _):
        here = pl.ds(pl.multiple_of(unit * unit_rows, unit_rows), unit_rows)
        preact = jnp.dot(x_ref[here, :], w_in_ref[...], preferred_element_type=jnp.float32) + b_in_ref[...]
        gate = jax.nn.sigmoid(preact)
        hidden_ref[here, :] = (preact * gate).astype(jnp.bfloat16)
        slope_ref[here, :] = gate * (1.0 + preact * (1.0 - gate))
        return 0

    lax.fori_loop(0, units, before, 0)
    sums[...] = jnp.zeros_like(sums)
    w_out_sum[...] = jnp.zeros_like(w_out_sum)

    nbr_copy.wait_recv()

    def foreign(q, _):
        tables(nbr_in[:, rows_of(q)], q, blocks + q)
        return 0

    lax.fori_loop(0, rim, foreign, 0)

    def relay(q):
        for owner, place in owned[q]:
            @pl.when(mode == owner)
            def _():
                total = outgoing[blocks + q].astype(jnp.float32)
                for hop in range(groups - 1):
                    pair_copy(blocks + q, 0, owner, place, hop).wait_recv()
                    total = total + far_in[hop, place].astype(jnp.float32)
                forward[place] = total.astype(jnp.bfloat16)
                relay_copy(place).start()

    def relay_copy(place):
        return pltpu.make_async_remote_copy(
            src_ref=forward.at[place], dst_ref=returned.at[place], send_sem=forward_send.at[place],
            recv_sem=returned_recv.at[place], device_id=(following, mode), device_id_type=MESH)

    for q in range(rim):
        rim_copies[q].wait_recv()
        weigh(blocks + q)

        def rim_product(tile, _):
            second = (tile + 1 + q) // (rim + 1)
            product(0, tile, blocks + q - rim * second, rim + q + tile)
            return 0

        lax.fori_loop(0, rim + 1, rim_product, 0)

        def rim_pick(eight, _):
            for part in range(4):
                rows, first, last = pick(0, 4 * eight + part, blocks + q, [(t, t) for t in range(rim - q)], None)
                firsts[rows, :] = first
                lasts[rows, :] = last
            for part in range(4):
                rows, first, last = pick(
                    0, 4 * eight + part, rim + q, [(rim - q + t, 2 * rim + t - q) for t in range(q + 1)], None)
                firsts[rows, :] += first
                lasts[rows, :] += last
            return 0

        lax.fori_loop(0, eights // 4, rim_pick, 0)
        pack(blocks + q)
        deliver(blocks + q, "start")
        pack(rim + q)
        deliver(rim + q, "start")
        if q:
            relay(q - 1)

    base = mode * share // TILE
    first_unit = mode * share // fold - base * (TILE // fold)

    def gather_block(place):
        total = outgoing[base + place].astype(jnp.float32)
        for hop in range(groups - 1):
            pltpu.make_async_remote_copy(
                src_ref=outgoing.at[0], dst_ref=own_in.at[hop, place], send_sem=pair_send.at[0, 0],
                recv_sem=own_recv.at[hop, place], device_id=(slab, peer_mode(1)), device_id_type=MESH).wait_recv()
            total = total + own_in[hop, place].astype(jnp.float32)
        total_first[place * TILE : (place + 1) * TILE, :] = total[0:TILE]
        total_last[place * (TILE // 8) * slot_count // 16 : (place + 1) * (TILE // 8) * slot_count // 16, :] = total[TILE:]

        @pl.when(mode < groups // 2)
        def _():
            relay_copy(place).wait_recv()
            more = returned[place].astype(jnp.float32)
            total_first[place * TILE : (place + 1) * TILE, :] += more[0:TILE]
            total_last[place * (TILE // 8) * slot_count // 16 : (place + 1) * (TILE // 8) * slot_count // 16, :] += more[TILE:]

    row = lax.broadcasted_iota(jnp.int32, (unit_rows, TILE), 0)
    lane = lax.broadcasted_iota(jnp.int32, (unit_rows, TILE), 1)

    def expand(block, mask):
        wide = jnp.broadcast_to(block[:, None, :], (fold, slot_count, TILE)).reshape(unit_rows, TILE)
        return jnp.where(mask, wide, 0.0).astype(jnp.bfloat16)

    def after(unit, _):
        keep = lax.rem(row, slot_count) == lax.rem(lane, slot_count)
        keep_last = keep & (row // (8 * slot_count) == lane // slot_count)
        here = pl.ds(pl.multiple_of(unit * unit_rows, unit_rows), unit_rows)
        first = total_first[pl.ds(pl.multiple_of((unit + first_unit) * fold, fold), fold), :]
        last = total_last[pl.ds(pl.multiple_of((unit + first_unit) * 8, 8), 8), :]
        spread = jnp.concatenate(
            [expand(first, keep), expand(jnp.concatenate([last] * (fold // 8), axis=0), keep_last)], axis=1)
        hidden_cot = jnp.dot(spread, w_rep_ref[...], preferred_element_type=jnp.float32)
        pre_cot = (hidden_cot * slope_ref[here, :]).astype(jnp.bfloat16)
        pre_ref[here, :] = pre_cot
        sums[0:features, :] += lax.dot_general(
            x_ref[here, :], pre_cot, (((0,), (0,)), ((), ())), preferred_element_type=jnp.float32)
        sums[features : features + 1, :] += jnp.sum(pre_cot.astype(jnp.float32), axis=0, keepdims=True)
        w_out_sum[...] += lax.dot_general(
            spread, hidden_ref[here, :], (((0,), (0,)), ((), ())), preferred_element_type=jnp.float32)
        return 0

    early = (width - 1) * (TILE // fold) - 1
    for place in range(width - 1):
        gather_block(place)
    lax.fori_loop(0, early, after, 0)
    relay(rim - 1)
    gather_block(width - 1)
    lax.fori_loop(early, units, after, 0)
    for part in range(9):
        end = (part + 1) * slot_count if part < 8 else 2 * TILE
        sums[features + 1 + part : features + 2 + part, :] = jnp.sum(
            w_out_sum[part * slot_count : end, :], axis=0, keepdims=True)

    for group in range(groups):
        sums_out[group] = sums[group * quarter : (group + 1) * quarter, :].astype(jnp.bfloat16)
    near = [pltpu.make_async_remote_copy(
        src_ref=sums_out.at[peer_mode(hop)], dst_ref=near_in.at[hop - 1], send_sem=near_send.at[hop - 1],
        recv_sem=near_recv.at[hop - 1], device_id=(slab, peer_mode(hop)), device_id_type=MESH)
        for hop in range(1, groups)]
    for copy in near:
        copy.start()
    for copy in near:
        copy.wait_recv()
    total = sums[pl.ds(pl.multiple_of(mode * quarter, 8), quarter), :]
    for hop in range(1, groups):
        total = total + near_in[hop - 1].astype(jnp.float32)
    mine[...] = total.astype(jnp.bfloat16)

    def slab_copy(hop):
        return pltpu.make_async_remote_copy(
            src_ref=mine, dst_ref=rounds.at[slab], send_sem=slab_send.at[hop],
            recv_sem=slab_recv.at[slab], device_id=(peer_slab(hop), mode), device_id_type=MESH)

    def slab_copy_from(hop):
        return pltpu.make_async_remote_copy(
            src_ref=mine, dst_ref=rounds.at[peer_slab(hop)], send_sem=slab_send.at[hop],
            recv_sem=slab_recv.at[peer_slab(hop)], device_id=(peer_slab(hop), mode), device_id_type=MESH)

    def send(hop, _):
        slab_copy(hop).start()
        return 0

    def settle(hop, _):
        slab_copy_from(hop).wait_recv()
        return 0

    def sent(hop, _):
        slab_copy(hop).wait_send()
        return 0

    lax.fori_loop(1, slabs, send, 0)
    rounds[slab] = mine[...]

    def finish(unit, _):
        here = pl.ds(pl.multiple_of(unit * unit_rows, unit_rows), unit_rows)
        grad_ref[here, :] = lax.dot_general(
            pre_ref[here, :], w_in_ref[...], (((1,), (1,)), ((), ())), preferred_element_type=jnp.float32
        ).astype(jnp.bfloat16)
        return 0

    lax.fori_loop(0, units, finish, 0)
    lax.fori_loop(1, slabs, settle, 0)
    summed[...] = lax.fori_loop(
        1, slabs, lambda index, value: value + rounds[index].astype(jnp.float32), rounds[0].astype(jnp.float32)
    ).astype(jnp.bfloat16)
    back = [pltpu.make_async_remote_copy(
        src_ref=summed, dst_ref=everyone.at[mode], send_sem=back_send.at[hop - 1],
        recv_sem=back_recv.at[hop - 1], device_id=(slab, peer_mode(hop)), device_id_type=MESH)
        for hop in range(1, groups)]
    back_from = [pltpu.make_async_remote_copy(
        src_ref=summed, dst_ref=everyone.at[peer_mode(groups - hop)], send_sem=back_send.at[hop - 1],
        recv_sem=back_recv.at[hop - 1], device_id=(slab, peer_mode(hop)), device_id_type=MESH)
        for hop in range(1, groups)]
    for copy in back:
        copy.start()
    everyone[mode] = summed[...]

    for copy in rim_copies:
        copy.wait_send()
    nbr_copy.wait_send()
    for block in range(blocks + rim):
        deliver(block, "sent")

    @pl.when(mode < groups // 2)
    def _():
        for place in range(width):
            relay_copy(place).wait_send()

    for copy in near:
        copy.wait_send()
    lax.fori_loop(1, slabs, sent, 0)

    for copy in back_from:
        copy.wait_recv()
    for copy in back:
        copy.wait_send()


def clip_kernel(raw_ref, grad_ref, grad_hbm, w_in_out, b_in_out, w_out_out, grad_sem):
    copy = pltpu.make_async_copy(grad_ref, grad_hbm, grad_sem.at[0])
    copy.start()
    features = w_in_out.shape[0]
    raw = jnp.concatenate([raw_ref[group].astype(jnp.float32) for group in range(raw_ref.shape[0])], axis=0)
    factor = jnp.minimum(1.0, CLIP_NORM / jnp.sqrt(jnp.sum(raw * raw, keepdims=True) + 1e-6))
    scaled = raw * factor
    w_in_out[...] = scaled[0:features, :]
    b_in_out[...] = scaled[features : features + 1, :].reshape(b_in_out.shape)
    w_out_out[...] = scaled[features + 1 : features + 10, :]
    copy.wait()


def shards(slabs, groups, eigvec, species, mode_cot, neighbours, pair_features, w_in, b_in, w_out):
    atoms, _, modes = eigvec.shape
    slot_count = neighbours.shape[1]
    features, hidden_width = w_in.shape
    pairs = pair_features.shape[0]
    blocks = atoms // TILE
    rim = blocks // 2
    fold = 8 * TILE // slot_count
    share = atoms // groups
    width = max(-(-(owner + 1) * share // TILE) - owner * share // TILE for owner in range(groups))
    lasts = TILE * slot_count // TILE
    everything = blocks + rim
    quarter = -(-(features + 10) // (groups * 16)) * 16
    bf16, f32, i32 = jnp.bfloat16, jnp.float32, jnp.int32
    dma = pltpu.SemaphoreType.DMA
    grads, raw = pl.pallas_call(
        functools.partial(kernel, slabs, groups),
        out_shape=(
            jax.ShapeDtypeStruct(pair_features.shape, bf16),
            jax.ShapeDtypeStruct((groups, quarter, hidden_width), bf16),
        ),
        in_specs=[ANY, VMEM, VMEM, VMEM, ANY, VMEM, VMEM, VMEM],
        out_specs=(VMEM, VMEM),
        scratch_shapes=[
            pltpu.VMEM((3, atoms, modes), bf16),
            pltpu.VMEM(pair_features.shape, bf16),
            pltpu.VMEM((1, atoms), i32),
            pltpu.VMEM((2 * TILE, hidden_width), bf16),
            pltpu.VMEM((3, everything * TILE, modes), bf16),
            pltpu.VMEM((3, everything * TILE, modes), bf16),
            pltpu.VMEM((slot_count, rim * TILE), i32),
            pltpu.VMEM((everything * TILE, TILE), i32),
            pltpu.VMEM((everything * TILE, TILE), i32),
            pltpu.VMEM((3 * rim + 1, 3 * TILE, 3 * TILE), f32),
            pltpu.VMEM((3 * rim + 1, 3 * TILE, 3 * TILE), f32),
            pltpu.VMEM((everything * TILE, TILE), f32),
            pltpu.VMEM((everything * TILE, TILE), f32),
            pltpu.VMEM((everything, TILE + lasts, TILE), bf16),
            pltpu.VMEM((groups - 1, width, TILE + lasts, TILE), bf16),
            pltpu.VMEM((groups - 1, width, TILE + lasts, TILE), bf16),
            pltpu.VMEM((width, TILE + lasts, TILE), bf16),
            pltpu.VMEM((width, TILE + lasts, TILE), bf16),
            pltpu.VMEM((width * TILE, TILE), f32),
            pltpu.VMEM((width * lasts, TILE), f32),
            pltpu.VMEM((pairs, hidden_width), bf16),
            pltpu.VMEM((pairs, hidden_width), f32),
            pltpu.VMEM((pairs, hidden_width), bf16),
            pltpu.VMEM((2 * TILE, hidden_width), f32),
            pltpu.VMEM((groups * quarter, hidden_width), f32),
            pltpu.VMEM((groups, quarter, hidden_width), bf16),
            pltpu.VMEM((groups - 1, quarter, hidden_width), bf16),
            pltpu.VMEM((quarter, hidden_width), bf16),
            pltpu.VMEM((slabs, quarter, hidden_width), bf16),
            pltpu.VMEM((quarter, hidden_width), bf16),
            dma((rim + 1,)), dma((1,)), dma((rim,)), dma((rim,)), dma((1,)), dma((1,)),
            dma((everything, 2)), dma((groups - 1, width)), dma((groups - 1, width)),
            dma((width,)), dma((width,)),
            dma((groups - 1,)), dma((groups - 1,)), dma((slabs,)), dma((slabs,)),
            dma((groups - 1,)), dma((groups - 1,)),
        ],
        compiler_params=pltpu.CompilerParams(
            collective_id=0, has_side_effects=True, vmem_limit_bytes=VMEM_LIMIT),
        name="phonon",
    )(jnp.transpose(eigvec, (1, 0, 2)), species, mode_cot[None, :], neighbours.T, pair_features,
      w_in, b_in[None, :], w_out)
    return pl.pallas_call(
        clip_kernel,
        out_shape=(
            jax.ShapeDtypeStruct(pair_features.shape, bf16),
            jax.ShapeDtypeStruct((features, hidden_width), f32),
            jax.ShapeDtypeStruct((hidden_width,), f32),
            jax.ShapeDtypeStruct((9, hidden_width), f32),
        ),
        in_specs=[VMEM, VMEM],
        out_specs=(ANY, VMEM, VMEM, VMEM),
        scratch_shapes=[dma((1,))],
        compiler_params=pltpu.CompilerParams(vmem_limit_bytes=8 * 1024 * 1024),
        name="clip",
    )(raw, grads)


def solution(mesh):
    return jax.shard_map(
        functools.partial(shards, mesh.shape["slab"], mesh.shape["mode"]),
        mesh=mesh,
        in_specs=(
            P("slab", None, "mode"),
            P("slab"),
            P("mode"),
            P("slab", None),
            P(("slab", "mode"), None),
            P(),
            P(),
            P(),
        ),
        out_specs=(P(("slab", "mode"), None), P(), P(), P()),
        check_vma=False,
    )
```

profile of v0, /device:TPU:0, one launch (start us, length us, event | category | flops | bytes accessed | tf_op | source)
XLA Modules:
  0.0 79.7 jit_solution(8776815829984527517)
XLA Ops:
  0.6 75.1 %phonon.1 = (bf16[5120,128]{1,0:T(8,128)(2,1)}, bf16[4,48,256]{2,1,0:T(8,128)(2,1)}) custom-call(bf16[3,1280,256]{2,1,0:T(8,128)(2,1)} %bitcast.4, s32[1280]{0:T(1024)} %species_ref.1, f32[1,256]{1,0:T(1,128)} %bitcast.6, s32[16,1280]{1,0:T(8,128)} %bitcast.5, bf16[5120,128]{1,0:T(8,128)(2,1)} %x_hbm.1, bf16[128,256]{1,0:T(8,128)(2,1)} %w_in_ref.1, ...), custom_call_target="tpu_custom_call" | custom-call | tf_op jit(solution)/shard_map/phonon/pallas_call | solution.py:476
  75.7 0.0 copy-start
  75.7 1.3 %copy-done = bf16[5120,128]{1,0:T(8,128)(2,1)S(1)} copy-done((bf16[5120,128]{1,0:T(8,128)(2,1)S(1)}, bf16[5120,128]{1,0:T(8,128)(2,1)}, u32[]{:S(2)}) %copy-start) | copy-done | bytes 1310744
  77.0 0.0 copy-start.1
  77.0 0.9 %copy-done.1 = bf16[4,48,256]{2,1,0:T(8,128)(2,1)S(1)} copy-done((bf16[4,48,256]{2,1,0:T(8,128)(2,1)S(1)}, bf16[4,48,256]{2,1,0:T(8,128)(2,1)}, u32[]{:S(2)}) %copy-start.1) | copy-done | bytes 98328
  77.9 1.8 %clip.1 = (bf16[5120,128]{1,0:T(8,128)(2,1)}, f32[128,256]{1,0:T(8,128)}, f32[256]{0:T(256)}, f32[9,256]{1,0:T(8,128)}) custom-call(bf16[4,48,256]{2,1,0:T(8,128)(2,1)S(1)} %copy-done.1, bf16[5120,128]{1,0:T(8,128)(2,1)S(1)} %copy-done), custom_call_target="tpu_custom_call" | custom-call | tf_op jit(solution)/shard_map/clip/pallas_call | solution.py:526
Async XLA Ops:
  75.7 1.3 %copy-start = (bf16[5120,128]{1,0:T(8,128)(2,1)S(1)}, bf16[5120,128]{1,0:T(8,128)(2,1)}, u32[]{:S(2)}) copy-start(bf16[5120,128]{1,0:T(8,128)(2,1)} %get-tuple-element.7.grad_ref) | copy-start | bytes 3932164
  77.0 0.9 %copy-start.1 = (bf16[4,48,256]{2,1,0:T(8,128)(2,1)S(1)}, bf16[4,48,256]{2,1,0:T(8,128)(2,1)}, u32[]{:S(2)}) copy-start(bf16[4,48,256]{2,1,0:T(8,128)(2,1)} %get-tuple-element.6.raw_ref) | copy-start | bytes 294916
where the time goes:
time: 79.9 us; the launch traced here: 79.7 us
  Pallas kernels  76.8 us (96%)
  local copies, waits for them, and re-layouts  2.2 us (3%)
    pallas_call x1, Pallas kernels, shards(): pl.pallas_call(functools.partial(kernel, slabs, groups), out_shape=(jax.S...  75.1 us
    unnamed x4, local copies, waits for them, and re-layouts  2.2 us
    pallas_call x1, Pallas kernels, shards(): pl.pallas_call(clip_kernel, out_shape=(jax.ShapeDtypeStruct(pair_features...  1.76 us

commit v1 on v0

--- a/solution.py
+++ b/solution.py
@@ -15,19 +15,20 @@
 MESH = pl.DeviceIdType.MESH
 VMEM = pl.BlockSpec(memory_space=pltpu.VMEM)
 ANY = pl.BlockSpec(memory_space=pl.ANY)
+HBM = pl.BlockSpec(memory_space=pltpu.HBM)
 
 
 def rows_of(block):
     return pl.ds(pl.multiple_of(block * TILE, TILE), TILE)
 
 
-def kernel(slabs, groups, eig_ref, species_ref, cot_ref, nbr_ref, x_hbm, w_in_ref, b_in_ref, w_out_ref,
-           grad_ref, everyone,
-           eig, x_ref, species_row, w_rep_ref, panel, weighted, nbr_in, low_ref, high_ref, even, odd, firsts, lasts, outgoing,
-           own_in, far_in, forward, returned, total_first, total_last, hidden_ref, slope_ref, pre_ref,
+def kernel(slabs, groups, eig_ref, species_hbm, cot_hbm, nbr_hbm, x_hbm, w_in_hbm, b_in_hbm, w_out_hbm,
+           grad_hbm, everyone,
+           species_ref, cot_ref, nbr_ref, w_in_ref, b_in_ref, w_out_ref, eig, x_ref, species_row, w_rep_ref, panel, weighted, nbr_in, low_ref, high_ref, even, odd, firsts, lasts, outgoing,
+           own_in, far_in, forward, returned, total_first, total_last, hidden_ref, slope_ref, pre_ref, grad_ref,
            w_out_sum, sums, sums_out, near_in, mine, rounds, summed,
-           eig_sem, x_sem, rim_send, rim_recv, nbr_send, nbr_recv, pair_send, own_recv, far_recv,
-           forward_send, returned_recv, near_send, near_recv, slab_send, slab_recv, back_send, back_recv):
+           small_sem, eig_sem, x_sem, rim_send, rim_recv, nbr_send, nbr_recv, pair_send, own_recv, far_recv,
+           forward_send, returned_recv, near_send, near_recv, slab_send, slab_recv, back_send, back_recv, grad_sem):
     slab, mode = lax.axis_index("slab"), lax.axis_index("mode")
     atoms = eig.shape[1]
     slot_count = nbr_ref.shape[0]
@@ -55,12 +56,16 @@
 
     previous, following = peer_slab(slabs - 1), peer_slab(1)
 
+    small = [pltpu.make_async_copy(source, target, small_sem.at[index]) for index, (source, target) in enumerate((
+        (species_hbm, species_ref), (nbr_hbm, nbr_ref), (cot_hbm, cot_ref), (w_in_hbm, w_in_ref),
+        (b_in_hbm, b_in_ref), (w_out_hbm, w_out_ref)))]
+    small[0].start()
     eig_copies = [pltpu.make_async_copy(
         eig_ref.at[:, block * TILE : (block + 1) * TILE, :], eig.at[:, block * TILE : (block + 1) * TILE, :],
         eig_sem.at[block]) for block in range(rim)]
     eig_copies.append(pltpu.make_async_copy(
         eig_ref.at[:, rim * TILE :, :], eig.at[:, rim * TILE :, :], eig_sem.at[rim]))
-    for copy in eig_copies:
+    for copy in eig_copies[0:1] + small[1:] + eig_copies[1:]:
         copy.start()
     x_copy = pltpu.make_async_copy(x_hbm, x_ref, x_sem.at[0])
     x_copy.start()
@@ -74,6 +79,7 @@
         return 0
 
     lax.fori_loop(1, slabs, greet, 0)
+    small[0].wait()
     species_row[...] = species_ref[...].reshape(species_row.shape)
     roots = [1.0 / math.sqrt(mass) for mass in MASS_TABLE]
 
@@ -111,12 +117,14 @@
     scale(0)
     pl.semaphore_wait(barrier, groups - 1 + slabs - 1)
     rim_copies[0].start()
+    small[1].wait()
     nbr_copy.start()
     for q in range(1, rim):
         eig_copies[q].wait()
         scale(q)
         rim_copies[q].start()
     eig_copies[rim].wait()
+    small[2].wait()
 
     def begin(block, _):
         scale(block)
@@ -182,10 +190,11 @@
             lasts[rows, :] = last
 
     def lead(tile, _):
-        own_product(0, tile)
-        return 0
-
-    lax.fori_loop(0, tiles, lead, 0)
+        own_product(0, 2 * tile)
+        own_product(0, 2 * tile + 1)
+        return 0
+
+    lax.fori_loop(0, tiles // 2, lead, 0)
     for pair in range(rim):
         def own_step(step, _):
             for half in range(2):
@@ -227,6 +236,8 @@
         pack(block)
         deliver(block, "start")
 
+    for copy in small[3:]:
+        copy.wait()
     for part in range(8):
         w_rep_ref[part * slot_count : (part + 1) * slot_count, :] = jnp.broadcast_to(
             w_out_ref[part : part + 1, :].astype(jnp.float32), (slot_count, w_rep_ref.shape[1])).astype(jnp.bfloat16)
@@ -276,12 +287,14 @@
         rim_copies[q].wait_recv()
         weigh(blocks + q)
 
-        def rim_product(tile, _):
-            second = (tile + 1 + q) // (rim + 1)
-            product(0, tile, blocks + q - rim * second, rim + q + tile)
+        def rim_product(step, _):
+            for half in range(2):
+                tile = 2 * step + half
+                second = (tile + 1 + q) // (rim + 1)
+                product(0, tile, blocks + q - rim * second, rim + q + tile)
             return 0
 
-        lax.fori_loop(0, rim + 1, rim_product, 0)
+        lax.fori_loop(0, (rim + 1) // 2, rim_product, 0)
 
         def rim_pick(eight, _):
             for part in range(4):
@@ -323,21 +336,19 @@
             total_first[place * TILE : (place + 1) * TILE, :] += more[0:TILE]
             total_last[place * (TILE // 8) * slot_count // 16 : (place + 1) * (TILE // 8) * slot_count // 16, :] += more[TILE:]
 
-    row = lax.broadcasted_iota(jnp.int32, (unit_rows, TILE), 0)
-    lane = lax.broadcasted_iota(jnp.int32, (unit_rows, TILE), 1)
-
-    def expand(block, mask):
-        wide = jnp.broadcast_to(block[:, None, :], (fold, slot_count, TILE)).reshape(unit_rows, TILE)
-        return jnp.where(mask, wide, 0.0).astype(jnp.bfloat16)
+    keep = (lax.broadcasted_iota(jnp.int32, (slot_count, TILE), 0)
+            == lax.rem(lax.broadcasted_iota(jnp.int32, (slot_count, TILE), 1), slot_count))
+
+    def expand(block):
+        wide = jnp.broadcast_to(block[:, None, :], (fold, slot_count, TILE))
+        return jnp.where(keep[None], wide, 0.0).reshape(unit_rows, TILE).astype(jnp.bfloat16)
 
     def after(unit, _):
-        keep = lax.rem(row, slot_count) == lax.rem(lane, slot_count)
-        keep_last = keep & (row // (8 * slot_count) == lane // slot_count)
         here = pl.ds(pl.multiple_of(unit * unit_rows, unit_rows), unit_rows)
         first = total_first[pl.ds(pl.multiple_of((unit + first_unit) * fold, fold), fold), :]
         last = total_last[pl.ds(pl.multiple_of((unit + first_unit) * 8, 8), 8), :]
-        spread = jnp.concatenate(
-            [expand(first, keep), expand(jnp.concatenate([last] * (fold // 8), axis=0), keep_last)], axis=1)
+        last = jnp.concatenate([jnp.where(position == p, last, 0.0) for p in range(fold // 8)], axis=0)
+        spread = jnp.concatenate([expand(first), expand(last)], axis=1)
         hidden_cot = jnp.dot(spread, w_rep_ref[...], preferred_element_type=jnp.float32)
         pre_cot = (hidden_cot * slope_ref[here, :]).astype(jnp.bfloat16)
         pre_ref[here, :] = pre_cot
@@ -351,8 +362,9 @@
     early = (width - 1) * (TILE // fold) - 1
     for place in range(width - 1):
         gather_block(place)
-    lax.fori_loop(0, early, after, 0)
+    lax.fori_loop(0, early - 1, after, 0)
     relay(rim - 1)
+    lax.fori_loop(early - 1, early, after, 0)
     gather_block(width - 1)
     lax.fori_loop(early, units, after, 0)
     for part in range(9):
@@ -400,11 +412,16 @@
     lax.fori_loop(1, slabs, send, 0)
     rounds[slab] = mine[...]
 
+    def grad_copy(unit):
+        here = pl.ds(pl.multiple_of(unit * unit_rows, unit_rows), unit_rows)
+        return pltpu.make_async_copy(grad_ref.at[here, :], grad_hbm.at[here, :], grad_sem.at[unit])
+
     def finish(unit, _):
         here = pl.ds(pl.multiple_of(unit * unit_rows, unit_rows), unit_rows)
         grad_ref[here, :] = lax.dot_general(
             pre_ref[here, :], w_in_ref[...], (((1,), (1,)), ((), ())), preferred_element_type=jnp.float32
         ).astype(jnp.bfloat16)
+        grad_copy(unit).start()
         return 0
 
     lax.fori_loop(0, units, finish, 0)
@@ -439,15 +456,29 @@
         copy.wait_send()
     lax.fori_loop(1, slabs, sent, 0)
 
+    def placed(unit, _):
+        grad_copy(unit).wait()
+        return 0
+
+    lax.fori_loop(0, units, placed, 0)
     for copy in back_from:
         copy.wait_recv()
     for copy in back:
         copy.wait_send()
 
 
-def clip_kernel(raw_ref, grad_ref, grad_hbm, w_in_out, b_in_out, w_out_out, grad_sem):
-    copy = pltpu.make_async_copy(grad_ref, grad_hbm, grad_sem.at[0])
-    copy.start()
+def clip_kernel(raw_ref, grad_in, grad_hbm, w_in_out, b_in_out, w_out_out, held, in_sem, out_sem):
+    pieces = in_sem.shape[0]
+    rows = held.shape[0] // pieces
+    incoming, outgoing = [], []
+    for piece in range(pieces):
+        here = pl.ds(piece * rows, rows)
+        incoming.append(pltpu.make_async_copy(grad_in.at[here, :], held.at[here, :], in_sem.at[piece]))
+        outgoing.append(pltpu.make_async_copy(held.at[here, :], grad_hbm.at[here, :], out_sem.at[piece]))
+        incoming[piece].start()
+    for coming, going in zip(incoming, outgoing):
+        coming.wait()
+        going.start()
     features = w_in_out.shape[0]
     raw = jnp.concatenate([raw_ref[group].astype(jnp.float32) for group in range(raw_ref.shape[0])], axis=0)
     factor = jnp.minimum(1.0, CLIP_NORM / jnp.sqrt(jnp.sum(raw * raw, keepdims=True) + 1e-6))
@@ -455,7 +486,8 @@
     w_in_out[...] = scaled[0:features, :]
     b_in_out[...] = scaled[features : features + 1, :].reshape(b_in_out.shape)
     w_out_out[...] = scaled[features + 1 : features + 10, :]
-    copy.wait()
+    for copy in outgoing:
+        copy.wait()
 
 
 def shards(slabs, groups, eigvec, species, mode_cot, neighbours, pair_features, w_in, b_in, w_out):
@@ -479,9 +511,15 @@
             jax.ShapeDtypeStruct(pair_features.shape, bf16),
             jax.ShapeDtypeStruct((groups, quarter, hidden_width), bf16),
         ),
-        in_specs=[ANY, VMEM, VMEM, VMEM, ANY, VMEM, VMEM, VMEM],
-        out_specs=(VMEM, VMEM),
+        in_specs=[HBM] * 8,
+        out_specs=(ANY, VMEM),
         scratch_shapes=[
+            pltpu.VMEM(species.shape, i32),
+            pltpu.VMEM((1, modes), f32),
+            pltpu.VMEM((slot_count, atoms), i32),
+            pltpu.VMEM(w_in.shape, bf16),
+            pltpu.VMEM((1, hidden_width), f32),
+            pltpu.VMEM(w_out.shape, bf16),
             pltpu.VMEM((3, atoms, modes), bf16),
             pltpu.VMEM(pair_features.shape, bf16),
             pltpu.VMEM((1, atoms), i32),
@@ -505,6 +543,7 @@
             pltpu.VMEM((pairs, hidden_width), bf16),
             pltpu.VMEM((pairs, hidden_width), f32),
             pltpu.VMEM((pairs, hidden_width), bf16),
+            pltpu.VMEM(pair_features.shape, bf16),
             pltpu.VMEM((2 * TILE, hidden_width), f32),
             pltpu.VMEM((groups * quarter, hidden_width), f32),
             pltpu.VMEM((groups, quarter, hidden_width), bf16),
@@ -512,11 +551,11 @@
             pltpu.VMEM((quarter, hidden_width), bf16),
             pltpu.VMEM((slabs, quarter, hidden_width), bf16),
             pltpu.VMEM((quarter, hidden_width), bf16),
-            dma((rim + 1,)), dma((1,)), dma((rim,)), dma((rim,)), dma((1,)), dma((1,)),
+            dma((6,)), dma((rim + 1,)), dma((1,)), dma((rim,)), dma((rim,)), dma((1,)), dma((1,)),
             dma((everything, 2)), dma((groups - 1, width)), dma((groups - 1, width)),
             dma((width,)), dma((width,)),
             dma((groups - 1,)), dma((groups - 1,)), dma((slabs,)), dma((slabs,)),
-            dma((groups - 1,)), dma((groups - 1,)),
+            dma((groups - 1,)), dma((groups - 1,)), dma((share // fold,)),
         ],
         compiler_params=pltpu.CompilerParams(
             collective_id=0, has_side_effects=True, vmem_limit_bytes=VMEM_LIMIT),
@@ -531,10 +570,10 @@
             jax.ShapeDtypeStruct((hidden_width,), f32),
             jax.ShapeDtypeStruct((9, hidden_width), f32),
         ),
-        in_specs=[VMEM, VMEM],
+        in_specs=[VMEM, ANY],
         out_specs=(ANY, VMEM, VMEM, VMEM),
-        scratch_shapes=[dma((1,))],
-        compiler_params=pltpu.CompilerParams(vmem_limit_bytes=8 * 1024 * 1024),
+        scratch_shapes=[pltpu.VMEM(pair_features.shape, bf16), dma((share // fold,)), dma((share // fold,))],
+        compiler_params=pltpu.CompilerParams(vmem_limit_bytes=VMEM_LIMIT),
         name="clip",
     )(raw, grads)
 

time: 79.9 us -> 73.3 us (0.917)
  Pallas kernels: 76.8 us -> 72.5 us
  local copies, waits for them, and re-layouts: 2.2 us -> 0 us
    pallas_call x1, Pallas kernels: 75.1 us -> 68.8 us  [shards(): pl.pallas_call(functools.partial(kernel, slabs, groups), out_shape=(jax.S...]
    unnamed x4 -> x0, local copies, waits for them, and re-layouts: 2.2 us -> none
    pallas_call x1, Pallas kernels: 1.76 us -> 3.64 us  [shards(): pl.pallas_call(clip_kernel, out_shape=(jax.ShapeDtypeStruct(pair_features...]
where the time goes in v1:
time: 73.3 us; the launch traced here: 73.1 us
  Pallas kernels  72.5 us (99%)
    pallas_call x1, Pallas kernels, shards(): pl.pallas_call(functools.partial(kernel, slabs, groups), out_shape=(jax.S...  68.8 us
    pallas_call x1, Pallas kernels, shards(): pl.pallas_call(clip_kernel, out_shape=(jax.ShapeDtypeStruct(pair_features...  3.64 us

profile of v1, /device:TPU:0, one launch (start us, length us, event | category | flops | bytes accessed | tf_op | source)
XLA Modules:
  0.0 73.1 jit_solution(16429211551345537356)
XLA Ops:
  0.6 68.8 %phonon.1 = (bf16[5120,128]{1,0:T(8,128)(2,1)}, bf16[4,48,256]{2,1,0:T(8,128)(2,1)}) custom-call(bf16[3,1280,256]{2,1,0:T(8,128)(2,1)} %bitcast.4, s32[1280]{0:T(1024)} %species_hbm.1, f32[1,256]{1,0:T(1,128)} %bitcast.6, s32[16,1280]{1,0:T(8,128)} %bitcast.5, bf16[5120,128]{1,0:T(8,128)(2,1)} %x_hbm.1, bf16[128,256]{1,0:T(8,128)(2,1)} %w_in_hbm.1, ...), custom_call_target="tpu_custom_call" | custom-call | tf_op jit(solution)/shard_map/phonon/pallas_call | solution.py:508
  69.5 3.6 %clip.1 = (bf16[5120,128]{1,0:T(8,128)(2,1)}, f32[128,256]{1,0:T(8,128)}, f32[256]{0:T(256)}, f32[9,256]{1,0:T(8,128)}) custom-call(bf16[4,48,256]{2,1,0:T(8,128)(2,1)} %get-tuple-element.6.raw_ref, bf16[5120,128]{1,0:T(8,128)(2,1)} %get-tuple-element.7.grad_in), custom_call_target="tpu_custom_call" | custom-call | tf_op jit(solution)/shard_map/clip/pallas_call | solution.py:565
